TPU v7x, 128 devices: a whole 4x4x4 slice. The times are simulated.
128 devices in a mesh: sub: 8 (over z, core), grp: 16 (over x, y).
Axes of the slice: x: 4, y: 4, z: 4, core: 2. Of those that a mesh axis runs over, the one named last changes fastest.
Arguments:
- schur: bfloat16 [512, 1024, 1024], P(('sub', 'grp')), as said below
- mortar: bfloat16 [512, 8, 128, 128], P(('sub', 'grp')), may hold values from -0.5 to 0.5
- partner: int32 [512, 4], P(('sub', 'grp')), may hold values from 0 to 15, as said below
- corner_map: int32 [512, 8], P(('sub', 'grp')), may hold values from 0 to 127
- coarse_inv: float32 [8, 128, 128], P('sub'), as said below
- load: float32 [512, 1024, 384], P(('sub', 'grp')), may hold values from -6 to 6
Outputs:
- solution: float32 [512, 1024, 384], P(('sub', 'grp'))
Inputs may be any that keep to these rules, and one draw needn't show every extreme that they name: `partner`: within the 4 subdomains of one device, the entries form a permutation of 0 to 15. `schur`: each matrix is symmetric positive definite. `coarse_inv`: each matrix is symmetric positive definite.
All inputs are finite; a program needn't handle non-finite values.
Results may differ from a plain program's by a relative error of at most 0.0025.
Values may be sent and summed in bfloat16 or wider, within the bound.
A program may use at most 128 MiB of HBM per device.

v0:
```python
import jax
import jax.numpy as jnp
from jax import lax
from jax.sharding import PartitionSpec as P

ITERS = 2


def shifted(block, axis, distance):
    devices = range(lax.axis_size(axis))
    route = [((i - distance) % len(devices), i) for i in devices]
    return lax.ppermute(block, axis, route)


def face_terms(direction, schur, mortar, partner):
    subdoms = direction.shape[0]
    order = direction.shape[1]
    columns = direction.shape[2]
    faces_all = mortar.shape[1]
    block = mortar.shape[2]
    half_faces = faces_all // 2
    dir_half = direction.astype(jnp.bfloat16)
    stiff = jnp.einsum("sij,sjr->sir", schur, dir_half, preferred_element_type=jnp.float32)
    face_rows = dir_half.reshape(subdoms, faces_all, block, columns)
    traces = jnp.einsum(
        "sfij,sfjr->sfir", mortar, face_rows, preferred_element_type=jnp.float32
    ).astype(jnp.bfloat16)
    upper = traces[:, :half_faces].reshape(subdoms * half_faces, block, columns)
    lower = traces[:, half_faces:].reshape(subdoms * half_faces, block, columns)
    mates = partner.reshape(-1)
    inverse = jnp.argsort(mates)
    reordered = jnp.take(upper, inverse, axis=0)
    lower_mate = shifted(reordered, "sub", 1)
    jump_lower = (lower.astype(jnp.float32) - lower_mate.astype(jnp.float32)).astype(jnp.bfloat16)
    above = shifted(lower, "sub", -1)
    upper_mate = jnp.take(above, mates, axis=0)
    jump_upper = (upper.astype(jnp.float32) - upper_mate.astype(jnp.float32)).astype(jnp.bfloat16)
    jump_all = jnp.concatenate(
        [
            jump_upper.reshape(subdoms, half_faces, block, columns),
            jump_lower.reshape(subdoms, half_faces, block, columns),
        ],
        axis=1,
    )
    pulled = jnp.einsum("sfji,sfjr->sfir", mortar, jump_all, preferred_element_type=jnp.float32)
    return stiff + pulled.reshape(subdoms, order, columns)


def squares(residual):
    return lax.psum(jnp.sum(residual * residual, axis=(0, 1)), ("sub", "grp"))


def on_device(schur, mortar, partner, corner_map, coarse_inv, load):
    order = load.shape[1]
    corner_count = corner_map.shape[1]
    coarse_count = coarse_inv.shape[1]
    stride = order // corner_count
    onehot = (corner_map[..., None] == jnp.arange(coarse_count, dtype=jnp.int32)).astype(
        jnp.float32
    )
    coarse_matrix = coarse_inv[0]
    solution = jnp.zeros_like(load)
    residual = load
    direction = load
    norm_now = squares(residual)
    for step in range(ITERS):
        partial_value = face_terms(direction, schur, mortar, partner)
        corners = direction[:, ::stride, :]
        local_sum = jnp.einsum("sco,scr->or", onehot, corners, precision=lax.Precision.HIGHEST)
        coarse_sum = lax.psum(local_sum.astype(jnp.bfloat16), "grp").astype(jnp.float32)
        coarse_val = jnp.dot(coarse_matrix, coarse_sum, precision=lax.Precision.HIGHEST)
        corner_add = jnp.einsum("sco,or->scr", onehot, coarse_val, precision=lax.Precision.HIGHEST)
        image = partial_value.at[:, ::stride, :].add(corner_add)
        curvature = lax.psum(jnp.sum(direction * image, axis=(0, 1)), ("sub", "grp"))
        image, curvature = (image, curvature)
        step_len = norm_now / curvature
        solution = solution + step_len * direction
        if step + 1 < ITERS:
            residual = residual - step_len * image
            norm_next = squares(residual)
            direction = residual + norm_next / norm_now * direction
            norm_now = norm_next
    return solution


def solution(mesh):
    return jax.shard_map(
        on_device,
        mesh=mesh,
        in_specs=(
            P(("sub", "grp"), None, None),
            P(("sub", "grp"), None, None, None),
            P(("sub", "grp"), None),
            P(("sub", "grp"), None),
            P("sub", None, None),
            P(("sub", "grp"), None, None),
        ),
        out_specs=P(("sub", "grp"), None, None),
        check_vma=False,
    )
```

profile of v0, /device:TPU:1, one launch (start us, length us, event | category | flops | bytes accessed | tf_op | source)
XLA Modules:
  0.0 520.1 jit_solution(5917532602240920158)
XLA Ops:
  6.5 5.6 %multiply_reduce_fusion.1 = (f32[384]{0:T(512)S(1)}, bf16[4,1024,384]{2,1,0:T(8,128)(2,1)S(1)}) fusion(f32[4,1024,384]{2,1,0:T(8,128)} %param.13), kind=kLoop, calls=%fused_computation.17 | loop fusion | flops 4718208 | bytes 9438720 | tf_op jit(solution)/shard_map/reduce_sum | solution.py:50
  20.0 2.8 broadcast_select_fusion.1
  24.4 2.8 slice.20
  28.6 82.6 %all-reduce.4.cloned.1.call-done = bf16[128,384]{1,0:T(8,128)(2,1)} async-done(((bf16[128,384]{1,0:T(8,128)(2,1)}), bf16[128,384]{1,0:T(8,128)(2,1)}) %all-reduce.4.cloned.1.call-update) | async-done | bytes 98320 | tf_op jit(solution)/shard_map/psum | solution.py:70
  112.7 3.3 gather_fusion
  123.9 6.9 %bitcast_add_fusion = f32[4,1024,384]{2,1,0:T(8,128)} fusion(f32[4,8,384,128]{2,3,1,0:T(8,128)S(1)} %fusion.3, bf16[4,1024,1024]{2,1,0:T(8,128)(2,1)S(1)} %bitcast.65, bf16[4,1024,384]{2,1,0:T(8,128)(2,1)S(1)} %copy-done.2), kind=kOutput, calls=%fused_computation.6 | convolution fusion | flops 3222798336 | bytes 24117248 | tf_op jit(solution)/shard_map/sij,sjr->sir/dot_general | solution.py:23
  130.8 9.5 %copy.24 = f32[4,1024,384]{2,0,1:T(4,128)} copy(f32[4,1024,384]{2,1,0:T(8,128)} %bitcast_add_fusion) | data formatting | bytes 12582912 | tf_op jit(solution)/shard_map/add | solution.py:46
  142.4 9.6 %fusion.2 = f32[384]{0:T(512)S(1)} fusion(f32[4,1024,384]{2,0,1:T(4,128)} %scatter_fusion, f32[4,1024,384]{2,1,0:T(8,128)} %param.13), kind=kLoop, calls=%fused_computation.13 | loop fusion | flops 3145344 | bytes 12584448 | tf_op jit(solution)/shard_map/reduce_sum | solution.py:74
  152.0 64.9 %all-reduce = (f32[384]{0:T(512)S(1)}, f32[384]{0:T(512)S(1)}) all-reduce(f32[384]{0:T(512)S(1)} %get-tuple-element.12, f32[384]{0:T(512)S(1)} %fusion.2), channel_id=1, replica_groups=mesh['sub'=8,'grp'=16] {'sub','grp'}, use_global_device_ids=true, to_apply=%region_1.0 | all-reduce | flops 768 | bytes 6144 | tf_op jit(solution)/shard_map/psum | solution.py:50
  216.9 5.5 %multiply_reduce_fusion = f32[384]{0:T(512)S(1)} fusion(f32[4,1024,384]{2,1,0:T(8,128)} %param.13, f32[4,1024,384]{2,0,1:T(4,128)} %scatter_fusion, f32[384]{0:T(512)S(1)} %div.9), kind=kLoop, calls=%fused_computation.16 | loop fusion | flops 6291072 | bytes 12585984 | tf_op jit(solution)/shard_map/reduce_sum | solution.py:50
  222.4 64.4 %psum.45 = f32[384]{0:T(512)S(1)} all-reduce(f32[384]{0:T(512)S(1)} %multiply_reduce_fusion), channel_id=1, replica_groups=mesh['sub'=8,'grp'=16] {'sub','grp'}, use_global_device_ids=true, to_apply=%region_8.10 | all-reduce | flops 384 | bytes 3072 | tf_op jit(solution)/shard_map/psum | solution.py:50
  286.8 7.1 %fusion.21 = (bf16[4,1024,384]{2,1,0:T(8,128)(2,1)S(1)}, f32[4,1024,384]{2,1,0:T(8,128)}) fusion(f32[4,1024,384]{2,1,0:T(8,128)} %param.13, f32[384]{0:T(512)S(1)} %div.10, f32[4,1024,384]{2,0,1:T(4,128)} %scatter_fusion, f32[384]{0:T(512)S(1)} %div.9), kind=kLoop, calls=%fused_computation.58 | loop fusion | flops 7864320 | bytes 22023168 | tf_op jit(solution)/shard_map/convert_element_type | solution.py:22
  302.7 2.8 slice.23
  306.5 78.2 %all-reduce.6.cloned.1.call-done = bf16[128,384]{1,0:T(8,128)(2,1)} async-done(((bf16[128,384]{1,0:T(8,128)(2,1)}), bf16[128,384]{1,0:T(8,128)(2,1)}) %all-reduce.6.cloned.1.call-update) | async-done | bytes 98320 | tf_op jit(solution)/shard_map/psum | solution.py:70
  386.1 3.5 subtract_convert_fusion
  392.2 3.3 gather_fusion.2
  395.5 3.1 subtract_convert_fusion.1
  401.3 5.1 fusion.7
  406.4 6.5 %copy.41 = f32[4,1024,384]{1,2,0:T(8,128)} copy(f32[4,1024,384]{2,1,0:T(8,128)} %bitcast.68) | data formatting | bytes 12582912 | tf_op jit(solution)/shard_map/reshape | solution.py:46
  413.0 12.4 %bitcast_add_fusion.1 = f32[4,1024,384]{1,2,0:T(8,128)} fusion(f32[4,1024,384]{1,2,0:T(8,128)} %copy.41, bf16[4,1024,384]{2,1,0:T(8,128)(2,1)} %copy-done.3, bf16[4,1024,1024]{2,1,0:T(8,128)(2,1)} %param.8), kind=kOutput, calls=%fused_computation.7 | convolution fusion | flops 3222798336 | bytes 24117248 | tf_op jit(solution)/shard_map/sij,sjr->sir/dot_general | solution.py:23
  425.3 7.7 %copy.34 = f32[4,1024,384]{2,0,1:T(4,128)} copy(f32[4,1024,384]{1,2,0:T(8,128)} %bitcast_add_fusion.1) | data formatting | bytes 12582912 | tf_op jit(solution)/shard_map/add | solution.py:46
  435.1 5.3 %fusion = f32[384]{0:T(512)S(1)} fusion(f32[4,1024,384]{2,1,0:T(8,128)} %get-tuple-element.11, f32[4,1024,384]{2,0,1:T(4,128)} %scatter_fusion.1), kind=kLoop, calls=%fused_computation.9 | loop fusion | flops 3145344 | bytes 12584448 | tf_op jit(solution)/shard_map/reduce_sum | solution.py:74
  440.3 64.9 %psum.47 = f32[384]{0:T(512)S(1)} all-reduce(f32[384]{0:T(512)S(1)} %fusion), channel_id=1, replica_groups=mesh['sub'=8,'grp'=16] {'sub','grp'}, use_global_device_ids=true, to_apply=%region_12.14 | all-reduce | flops 384 | bytes 3072 | tf_op jit(solution)/shard_map/psum | solution.py:74
  505.2 8.0 %multiply_add_fusion = f32[4,1024,384]{2,1,0:T(8,128)} fusion(f32[4,1024,384]{2,1,0:T(8,128)} %get-tuple-element.11, f32[4,1024,384]{2,1,0:T(8,128)} %param.13, f32[384]{0:T(512)S(1)} %div.11, f32[384]{0:T(512)S(1)} %div.9), kind=kLoop, calls=%fused_computation.14 | loop fusion | flops 4718592 | bytes 18877440 | tf_op jit(solution)/shard_map/add | solution.py:77
  (68 shorter events, 40.6 us)
Async XLA Ops:
  6.5 5.6 %copy-start = (bf16[4,8,128,128]{3,2,1,0:T(8,128)(2,1)S(1)}, bf16[4,8,128,128]{3,2,1,0:T(8,128)(2,1)}, u32[]{:S(2)}) copy-start(bf16[4,8,128,128]{3,2,1,0:T(8,128)(2,1)} %param.9) | copy-start | bytes 3145732
  6.5 104.7 %all-reduce.4.cloned.1.call-start = ((), (), s32[]{:S(2)}) async-start(), calls=%async_computation | async-start | bytes 196608 | tf_op jit(solution)/shard_map/psum | solution.py:70
  12.2 1.7 copy-start.1
  13.8 3.0 copy-start.7
  15.4 97.3 %collective-permute-start = (bf16[16,128,384]{2,1,0:T(8,128)(2,1)}, bf16[16,128,384]{2,1,0:T(8,128)(2,1)}, u32[]{:S(2)}, u32[]{:S(2)}) collective-permute-start(bf16[16,128,384]{2,1,0:T(8,128)(2,1)} %bitcast.2), channel_id=1, source_target_pairs={{16,0},{32,16},{48,32},{64,48},{80,64},{96,80},{112,96},{0,112},{1... | collective-permute-start | bytes 4718600 | tf_op jit(solution)/shard_map/ppermute | solution.py:12
  18.1 9.2 %copy-start.6 = (s32[4,8]{1,0:T(4,128)S(1)}, s32[4,8]{1,0:T(4,128)}, u32[]{:S(2)}) copy-start(s32[4,8]{1,0:T(4,128)} %param.11) | copy-start | bytes 388
  18.1 93.1 %copy-start.5 = (f32[1,128,128]{2,1,0:T(8,128)S(1)}, f32[1,128,128]{2,1,0:T(8,128)}, u32[]{:S(2)}) copy-start(f32[1,128,128]{2,1,0:T(8,128)} %param.12) | copy-start | bytes 196612
  22.8 95.3 %collective-permute-start.1 = (bf16[16,128,384]{2,1,0:T(8,128)(2,1)}, bf16[16,128,384]{2,1,0:T(8,128)(2,1)}, u32[]{:S(2)}, u32[]{:S(2)}) collective-permute-start(bf16[16,128,384]{2,1,0:T(8,128)(2,1)} %broadcast_select_fusion.1), channel_id=1, source_target_pairs={{112,0},{0,16},{16,32},{32,48},{48,64},{64,80},{80,96},{96,112},{1... | collective-permute-start | bytes 4718600 | tf_op jit(solution)/shard_map/ppermute | solution.py:12
  28.3 356.4 %all-reduce.6.cloned.1.call-start = ((), (), s32[]{:S(2)}) async-start(), calls=%async_computation.1 | async-start | bytes 196608 | tf_op jit(solution)/shard_map/psum | solution.py:70
  118.2 3.6 slice-start
  120.7 2.3 slice-start.1
  120.7 3.2 copy-start.2
  293.9 1.7 copy-start.3
  301.7 84.4 %collective-permute-start.3 = (bf16[16,128,384]{1,2,0:T(8,128)(2,1)}, bf16[16,128,384]{1,2,0:T(8,128)(2,1)}, u32[]{:S(2)}, u32[]{:S(2)}) collective-permute-start(bf16[16,128,384]{1,2,0:T(8,128)(2,1)} %broadcast_select_fusion), channel_id=1, source_target_pairs={{112,0},{0,16},{16,32},{32,48},{48,64},{64,80},{80,96},{96,112},{1... | collective-permute-start | bytes 4718600 | tf_op jit(solution)/shard_map/ppermute | solution.py:12
  301.7 90.5 %collective-permute-start.2 = (bf16[16,128,384]{1,2,0:T(8,128)(2,1)}, bf16[16,128,384]{1,2,0:T(8,128)(2,1)}, u32[]{:S(2)}, u32[]{:S(2)}) collective-permute-start(bf16[16,128,384]{1,2,0:T(8,128)(2,1)} %bitcast.16), channel_id=1, source_target_pairs={{16,0},{32,16},{48,32},{64,48},{80,64},{96,80},{112,96},{0,112},{1... | collective-permute-start | bytes 4718600 | tf_op jit(solution)/shard_map/ppermute | solution.py:12
  398.7 2.7 copy-start.4
Sparse Core Ops, SparseCore 0:
  28.4 82.7 all-reduce.3
  306.6 77.9 all-reduce.5
where the time goes:
time: 521 us; the launch traced here: 520 us
  blocking collectives  194 us (37%)
  waiting for transfers between devices  161 us (31%)
  other arithmetic  63.4 us (12%)
  local copies, waits for them, and re-layouts  51.5 us (10%)
  matrix products  32.3 us (6%)
  between operations  13.6 us (3%)
    psum x2, waiting for transfers between devices, on_device(): lax.psum(local_sum.astype(jnp.bfloat16), 'grp').astype(jnp.float32)  161 us
    psum x2, blocking collectives, squares(): return lax.psum(jnp.sum(residual * residual, axis=(0, 1)), ('sub', 'grp'))  129 us
    psum x1, blocking collectives, on_device(): lax.psum(jnp.sum(direction * image, axis=(0, 1)), ('sub', 'grp'))  64.9 us
    dot_general x2, matrix products, face_terms(): jnp.einsum('sij,sjr->sir', schur, dir_half, preferred_element_type=jnp.fl...  19.3 us
    add x2, local copies, waits for them, and re-layouts, face_terms(): return stiff + pulled.reshape(subdoms, order, columns)  17.1 us
    reduce_sum x2, other arithmetic, on_device(): jnp.sum(direction * image, axis=(0, 1))  14.9 us
    reduce_sum x2, other arithmetic, squares(): return lax.psum(jnp.sum(residual * residual, axis=(0, 1)), ('sub', 'grp'))  11.1 us
  transfers between devices with their start and end apart: 6, of which 2 were waited for; matrix products, arithmetic and copies ran while one was open for 5% of the time, Pallas kernels for 0%

commit v1 on v0

--- a/solution.py
+++ b/solution.py
@@ -47,7 +47,9 @@
 
 
 def squares(residual):
-    return lax.psum(jnp.sum(residual * residual, axis=(0, 1)), ("sub", "grp"))
+    return jnp.sum(
+        lax.all_gather(jnp.sum(residual * residual, axis=(0, 1)), ("sub", "grp")), axis=0
+    )
 
 
 def on_device(schur, mortar, partner, corner_map, coarse_inv, load):

time: 521 us -> 514 us (0.987)
  waiting for transfers between devices: 161 us -> 91.9 us
  blocking collectives: 194 us -> 256 us
    psum x2 -> x0, blocking collectives: 129 us -> none  [squares(): return lax.psum(jnp.sum(residual * residual, axis=(0, 1)), ('sub', 'grp'))]
    all_gather x0 -> x2, blocking collectives: none -> 126 us  [squares(): lax.all_gather(jnp.sum(residual * residual, axis=(0, 1)), ('sub', 'grp'))]
    psum x2, waiting for transfers between devices: 161 us -> 91.8 us  [on_device(): lax.psum(local_sum.astype(jnp.bfloat16), 'grp').astype(jnp.float32)]
    psum x1 -> x2, blocking collectives: 64.9 us -> 130 us  [on_device(): lax.psum(jnp.sum(direction * image, axis=(0, 1)), ('sub', 'grp'))]
    reduce_sum x2 -> x4, other arithmetic: 11.1 us -> 11.5 us  [the longest x2 11.1 us: squares(): jnp.sum(residual * residual, axis=(0, 1))]
  transfers between devices with their start and end apart: 6 -> 6, of which waited for: 2 -> 2; matrix products, arithmetic and copies ran while one was open for 5% -> 6% of each run, Pallas kernels for 0% -> 0%
where the time goes in v1:
time: 514 us; the launch traced here: 513 us
  blocking collectives  256 us (50%)
  waiting for transfers between devices  91.9 us (18%)
  other arithmetic  64 us (12%)
  local copies, waits for them, and re-layouts  51.5 us (10%)
  matrix products  32.3 us (6%)
  between operations  13.6 us (3%)
    psum x2, blocking collectives, on_device(): lax.psum(jnp.sum(direction * image, axis=(0, 1)), ('sub', 'grp'))  130 us
    all_gather x2, blocking collectives, squares(): lax.all_gather(jnp.sum(residual * residual, axis=(0, 1)), ('sub', 'grp'))  126 us
    psum x2, waiting for transfers between devices, on_device(): lax.psum(local_sum.astype(jnp.bfloat16), 'grp').astype(jnp.float32)  91.8 us
    dot_general x2, matrix products, face_terms(): jnp.einsum('sij,sjr->sir', schur, dir_half, preferred_element_type=jnp.fl...  19.3 us
    add x2, local copies, waits for them, and re-layouts, face_terms(): return stiff + pulled.reshape(subdoms, order, columns)  17.1 us
    reduce_sum x2, other arithmetic, on_device(): jnp.sum(direction * image, axis=(0, 1))  14.9 us
    reduce_sum x2, other arithmetic, squares(): jnp.sum(residual * residual, axis=(0, 1))  11.1 us
  transfers between devices with their start and end apart: 6, of which 2 were waited for; matrix products, arithmetic and copies ran while one was open for 6% of the time, Pallas kernels for 0%

profile of v1, /device:TPU:1, one launch (start us, length us, event | category | flops | bytes accessed | tf_op | source)
XLA Modules:
  0.0 513.1 jit_solution(12769347194864861683)
XLA Ops:
  6.5 5.6 %multiply_reduce_fusion.1 = (f32[384]{0:T(512)S(1)}, bf16[4,1024,384]{2,1,0:T(8,128)(2,1)S(1)}) fusion(f32[4,1024,384]{2,1,0:T(8,128)} %param.13), kind=kLoop, calls=%fused_computation.17 | loop fusion | flops 4718208 | bytes 9438720 | tf_op jit(solution)/shard_map/reduce_sum | solution.py:51
  24.4 2.8 slice.20
  28.3 69.3 %all-gather.2 = f32[128,1,384]{2,1,0:T(1,128)S(1)} all-gather(f32[1,1,384]{2,1,0:T(1,128)S(1)} %reshape.127), channel_id=2, replica_groups=mesh['sub'=8,'grp'=16] {'sub','grp'}, dimensions={0}, use_global_device_ids=true | all-gather | bytes 198144 | tf_op jit(solution)/shard_map/all_gather | solution.py:51
  97.9 13.3 %all-reduce.3.cloned.1.call-done = bf16[128,384]{1,0:T(8,128)(2,1)} async-done(((bf16[128,384]{1,0:T(8,128)(2,1)}), bf16[128,384]{1,0:T(8,128)(2,1)}) %all-reduce.3.cloned.1.call-update) | async-done | bytes 98320 | tf_op jit(solution)/shard_map/psum | solution.py:72
  112.7 3.3 gather_fusion
  123.9 6.9 %bitcast_add_fusion = f32[4,1024,384]{2,1,0:T(8,128)} fusion(f32[4,8,384,128]{2,3,1,0:T(8,128)S(1)} %fusion.3, bf16[4,1024,1024]{2,1,0:T(8,128)(2,1)S(1)} %bitcast.65, bf16[4,1024,384]{2,1,0:T(8,128)(2,1)S(1)} %copy-done.2), kind=kOutput, calls=%fused_computation.6 | convolution fusion | flops 3222798336 | bytes 24117248 | tf_op jit(solution)/shard_map/sij,sjr->sir/dot_general | solution.py:23
  130.8 9.5 %copy.40 = f32[4,1024,384]{2,0,1:T(4,128)} copy(f32[4,1024,384]{2,1,0:T(8,128)} %bitcast_add_fusion) | data formatting | bytes 12582912 | tf_op jit(solution)/shard_map/add | solution.py:46
  142.4 9.6 %fusion.2 = f32[384]{0:T(512)S(1)} fusion(f32[4,1024,384]{2,0,1:T(4,128)} %scatter_fusion, f32[4,1024,384]{2,1,0:T(8,128)} %param.13), kind=kLoop, calls=%fused_computation.13 | loop fusion | flops 3145344 | bytes 12584448 | tf_op jit(solution)/shard_map/reduce_sum | solution.py:76
  152.0 64.9 %psum.29 = f32[384]{0:T(512)S(1)} all-reduce(f32[384]{0:T(512)S(1)} %fusion.2), channel_id=1, replica_groups=mesh['sub'=8,'grp'=16] {'sub','grp'}, use_global_device_ids=true, to_apply=%region_6.8 | all-reduce | flops 384 | bytes 3072 | tf_op jit(solution)/shard_map/psum | solution.py:76
  216.9 5.5 %multiply_reduce_fusion = f32[384]{0:T(512)S(1)} fusion(f32[4,1024,384]{2,1,0:T(8,128)} %param.13, f32[4,1024,384]{2,0,1:T(4,128)} %scatter_fusion, f32[384]{0:T(512)S(1)} %div.13), kind=kLoop, calls=%fused_computation.16 | loop fusion | flops 6291072 | bytes 12585984 | tf_op jit(solution)/shard_map/reduce_sum | solution.py:51
  222.4 56.9 %all-gather.3 = f32[128,1,384]{2,1,0:T(1,128)S(1)} all-gather(f32[1,1,384]{2,1,0:T(1,128)S(1)} %reshape.129), channel_id=3, replica_groups=mesh['sub'=8,'grp'=16] {'sub','grp'}, dimensions={0}, use_global_device_ids=true | all-gather | bytes 198144 | tf_op jit(solution)/shard_map/all_gather | solution.py:51
  279.5 7.4 %fusion.21 = (bf16[4,1024,384]{2,1,0:T(8,128)(2,1)S(1)}, f32[4,1024,384]{2,1,0:T(8,128)}) fusion(f32[4,1024,384]{2,1,0:T(8,128)} %param.13, f32[384]{0:T(512)S(1)} %div.14, f32[4,1024,384]{2,0,1:T(4,128)} %scatter_fusion, f32[384]{0:T(512)S(1)} %div.13), kind=kLoop, calls=%fused_computation.58 | loop fusion | flops 7864320 | bytes 22023168 | tf_op jit(solution)/shard_map/convert_element_type | solution.py:22
  295.4 2.8 slice.23
  299.2 78.5 %all-reduce.5.cloned.1.call-done = bf16[128,384]{1,0:T(8,128)(2,1)} async-done(((bf16[128,384]{1,0:T(8,128)(2,1)}), bf16[128,384]{1,0:T(8,128)(2,1)}) %all-reduce.5.cloned.1.call-update) | async-done | bytes 98320 | tf_op jit(solution)/shard_map/psum | solution.py:72
  379.2 3.5 subtract_convert_fusion
  385.2 3.3 gather_fusion.2
  388.5 3.1 subtract_convert_fusion.1
  394.4 5.1 fusion.7
  399.5 6.5 %copy.57 = f32[4,1024,384]{1,2,0:T(8,128)} copy(f32[4,1024,384]{2,1,0:T(8,128)} %bitcast.68) | data formatting | bytes 12582912 | tf_op jit(solution)/shard_map/reshape | solution.py:46
  406.0 12.4 %bitcast_add_fusion.1 = f32[4,1024,384]{1,2,0:T(8,128)} fusion(f32[4,1024,384]{1,2,0:T(8,128)} %copy.57, bf16[4,1024,384]{2,1,0:T(8,128)(2,1)} %copy-done.3, bf16[4,1024,1024]{2,1,0:T(8,128)(2,1)} %param.8), kind=kOutput, calls=%fused_computation.7 | convolution fusion | flops 3222798336 | bytes 24117248 | tf_op jit(solution)/shard_map/sij,sjr->sir/dot_general | solution.py:23
  418.4 7.7 %copy.50 = f32[4,1024,384]{2,0,1:T(4,128)} copy(f32[4,1024,384]{1,2,0:T(8,128)} %bitcast_add_fusion.1) | data formatting | bytes 12582912 | tf_op jit(solution)/shard_map/add | solution.py:46
  428.1 5.3 %fusion = f32[384]{0:T(512)S(1)} fusion(f32[4,1024,384]{2,1,0:T(8,128)} %get-tuple-element.9, f32[4,1024,384]{2,0,1:T(4,128)} %scatter_fusion.1), kind=kLoop, calls=%fused_computation.9 | loop fusion | flops 3145344 | bytes 12584448 | tf_op jit(solution)/shard_map/reduce_sum | solution.py:76
  433.4 64.9 %psum.31 = f32[384]{0:T(512)S(1)} all-reduce(f32[384]{0:T(512)S(1)} %fusion), channel_id=1, replica_groups=mesh['sub'=8,'grp'=16] {'sub','grp'}, use_global_device_ids=true, to_apply=%region_12.14 | all-reduce | flops 384 | bytes 3072 | tf_op jit(solution)/shard_map/psum | solution.py:76
  498.3 8.0 %multiply_add_fusion = f32[4,1024,384]{2,1,0:T(8,128)} fusion(f32[4,1024,384]{2,1,0:T(8,128)} %get-tuple-element.9, f32[4,1024,384]{2,1,0:T(8,128)} %param.13, f32[384]{0:T(512)S(1)} %div.15, f32[384]{0:T(512)S(1)} %div.13), kind=kLoop, calls=%fused_computation.14 | loop fusion | flops 4718592 | bytes 18877440 | tf_op jit(solution)/shard_map/add | solution.py:79
  (73 shorter events, 43.3 us)
Async XLA Ops:
  6.5 5.6 %copy-start = (bf16[4,8,128,128]{3,2,1,0:T(8,128)(2,1)S(1)}, bf16[4,8,128,128]{3,2,1,0:T(8,128)(2,1)}, u32[]{:S(2)}) copy-start(bf16[4,8,128,128]{3,2,1,0:T(8,128)(2,1)} %param.9) | copy-start | bytes 3145732
  6.5 104.7 %all-reduce.3.cloned.1.call-start = ((), (), s32[]{:S(2)}) async-start(), calls=%async_computation | async-start | bytes 196608 | tf_op jit(solution)/shard_map/psum | solution.py:72
  12.2 1.7 copy-start.1
  13.8 3.0 copy-start.7
  15.4 97.3 %collective-permute-start = (bf16[16,128,384]{2,1,0:T(8,128)(2,1)}, bf16[16,128,384]{2,1,0:T(8,128)(2,1)}, u32[]{:S(2)}, u32[]{:S(2)}) collective-permute-start(bf16[16,128,384]{2,1,0:T(8,128)(2,1)} %bitcast.2), channel_id=1, source_target_pairs={{16,0},{32,16},{48,32},{64,48},{80,64},{96,80},{112,96},{0,112},{1... | collective-permute-start | bytes 4718600 | tf_op jit(solution)/shard_map/ppermute | solution.py:12
  18.1 9.2 %copy-start.6 = (s32[4,8]{1,0:T(4,128)S(1)}, s32[4,8]{1,0:T(4,128)}, u32[]{:S(2)}) copy-start(s32[4,8]{1,0:T(4,128)} %param.11) | copy-start | bytes 388
  18.1 93.1 %copy-start.5 = (f32[1,128,128]{2,1,0:T(8,128)S(1)}, f32[1,128,128]{2,1,0:T(8,128)}, u32[]{:S(2)}) copy-start(f32[1,128,128]{2,1,0:T(8,128)} %param.12) | copy-start | bytes 196612
  22.8 95.3 %collective-permute-start.1 = (bf16[16,128,384]{2,1,0:T(8,128)(2,1)}, bf16[16,128,384]{2,1,0:T(8,128)(2,1)}, u32[]{:S(2)}, u32[]{:S(2)}) collective-permute-start(bf16[16,128,384]{2,1,0:T(8,128)(2,1)} %broadcast_select_fusion.1), channel_id=1, source_target_pairs={{112,0},{0,16},{16,32},{32,48},{48,64},{64,80},{80,96},{96,112},{1... | collective-permute-start | bytes 4718600 | tf_op jit(solution)/shard_map/ppermute | solution.py:12
  28.3 349.4 %all-reduce.5.cloned.1.call-start = ((), (), s32[]{:S(2)}) async-start(), calls=%async_computation.1 | async-start | bytes 196608 | tf_op jit(solution)/shard_map/psum | solution.py:72
  118.2 3.6 slice-start
  120.7 2.3 slice-start.1
  120.7 3.2 copy-start.2
  286.9 1.7 copy-start.3
  294.7 84.5 %collective-permute-start.3 = (bf16[16,128,384]{1,2,0:T(8,128)(2,1)}, bf16[16,128,384]{1,2,0:T(8,128)(2,1)}, u32[]{:S(2)}, u32[]{:S(2)}) collective-permute-start(bf16[16,128,384]{1,2,0:T(8,128)(2,1)} %broadcast_select_fusion), channel_id=1, source_target_pairs={{112,0},{0,16},{16,32},{32,48},{48,64},{64,80},{80,96},{96,112},{1... | collective-permute-start | bytes 4718600 | tf_op jit(solution)/shard_map/ppermute | solution.py:12
  294.7 90.6 %collective-permute-start.2 = (bf16[16,128,384]{1,2,0:T(8,128)(2,1)}, bf16[16,128,384]{1,2,0:T(8,128)(2,1)}, u32[]{:S(2)}, u32[]{:S(2)}) collective-permute-start(bf16[16,128,384]{1,2,0:T(8,128)(2,1)} %bitcast.16), channel_id=1, source_target_pairs={{16,0},{32,16},{48,32},{64,48},{80,64},{96,80},{112,96},{0,112},{1... | collective-permute-start | bytes 4718600 | tf_op jit(solution)/shard_map/ppermute | solution.py:12
  391.7 2.7 copy-start.4
Sparse Core Ops, SparseCore 0:
  28.4 82.7 all-reduce.2
  299.3 78.3 all-reduce.4
